TPU v7x, 256 devices: a whole 4x4x8 slice. The times are simulated.
256 devices in a mesh: layer: 32 (over y, z_lo, core), dp: 8 (over z_hi, x).
Axes of the slice: x: 4, y: 4, z: 8 (z_hi: 2, z_lo: 4; z = z_hi * 4 + z_lo), core: 2. Of those that a mesh axis runs over, the one named last changes fastest.
Arguments:
- acts: bfloat16 [8192, 32768], P('dp', 'layer'), may hold values from -6 to 6
- grads: bfloat16 [8192, 32768], P('dp', 'layer'), may hold values from -6 to 6
Outputs:
- act_diag: float32 [1024, 32768], P('dp', 'layer')
- grad_diag: float32 [1024, 32768], P('dp', 'layer')
- act_cross: float32 [1024, 32768], P('dp', 'layer')
- grad_cross: float32 [1024, 32768], P('dp', 'layer')
All inputs are finite; a program needn't handle non-finite values.
Results may differ from a plain program's by a relative error of at most 0.0003.
Values may be sent and summed in bfloat16 or wider, within the bound.
No kernel may reach another device: no remote copies, remote signals or barrier semaphores. Data moves between devices by JAX's collectives and lax.ppermute only.
A program may use at most 128 MiB of HBM per device.

v0:
```python
import jax
import jax.numpy as jnp
from jax import lax
from jax.experimental import pallas as pl
from jax.experimental.pallas import tpu as pltpu
from jax.sharding import PartitionSpec as P


D = 8192
BLK = 128
LANES = 128
HEAD = 16
RING = 4
POWER = 25
SPAN = 1024.0
BASE = 2.0**-5


VMEM = pl.BlockSpec(memory_space=pltpu.VMEM)
SMEM = pl.BlockSpec(memory_space=pltpu.SMEM)
STEP = 32


def unit_of(bound):
    unit = bound * jnp.float32(1.01 / SPAN) + jnp.float32(1e-30)
    return unit.astype(jnp.bfloat16)


def encode(value, gain):
    scaled = value * gain
    lifted = scaled + jnp.where(scaled < 0, jnp.float32(-BASE), jnp.float32(BASE))
    two = lifted * lifted
    four = two * two
    eight = four * four
    return (eight * eight * eight * lifted).astype(jnp.bfloat16)


def decode(code, unit):
    wide = code.astype(jnp.float32)
    size = jnp.maximum(jnp.abs(wide), jnp.float32(BASE**POWER))
    root = jnp.exp2(jnp.log2(size) * jnp.float32(1.0 / POWER) + jnp.float32(5.0))
    grown = root - 1.0
    return jnp.where(wide < 0, -grown, grown) * unit


def lanes_of(unit, rows):
    return jnp.broadcast_to(unit[0:1, :], (rows, LANES))


def head_of(message):
    return message[0:HEAD, :].astype(jnp.float32)[0:8, :]


def block_at(message, piece, groups, group, row):
    start = HEAD + (piece * groups + group) * BLK
    return message[pl.ds(start + row, STEP), :]


def write_head(message, unit):
    message[0:HEAD, :] = jnp.broadcast_to(unit[0:1, :], (HEAD, LANES))


def largest(ref, start, rows, groups):
    def body(i, most):
        for r in range(STEP // 8):
            for g in range(groups):
                part = ref[pl.ds(start + i * STEP + r * 8, 8), pl.ds(g * LANES, LANES)]
                most = jnp.maximum(most, jnp.abs(part))
        return most

    most = lax.fori_loop(0, rows // STEP, body, jnp.zeros((8, LANES), jnp.float32))
    return jnp.broadcast_to(jnp.max(most, keepdims=True), (8, LANES))


def gain_of(unit):
    return jnp.float32(BASE) / unit.astype(jnp.float32)


def fill(message, piece, groups, gain, source):
    wide = lanes_of(gain, STEP)

    def body(i, carry):
        row = pl.multiple_of(i * STEP, STEP)
        for g in range(groups):
            start = HEAD + (piece * groups + g) * BLK
            message[pl.ds(start + row, STEP), :] = encode(source(row, g), wide)
        return carry

    lax.fori_loop(0, BLK // STEP, body, 0)


def rows_of(owner):
    return pl.multiple_of(owner * BLK, BLK)


def around(x, by):
    return lax.rem(x + by + RING, RING)


def tile(ref, start, row, g):
    return ref[pl.ds(start + row, STEP), pl.ds(g * LANES, LANES)]


def first_kernel(at, total, plus, minus, most):
    groups = total.shape[1] // LANES
    x = at[0]
    bound = largest(total, 0, total.shape[0], groups)
    most[...] = bound
    unit = unit_of(bound)
    gain = gain_of(unit)
    write_head(plus, unit)
    write_head(minus, unit)
    far, right, left = around(x, 2), around(x, 1), around(x, -1)
    for message, piece, owner in (
        (plus, 0, far),
        (minus, 0, RING + far),
        (plus, 1, RING + right),
        (minus, 1, left),
    ):
        start = rows_of(owner)
        fill(message, piece, groups, gain, lambda row, g, start=start: tile(total, start, row, g))


def second_kernel(at, total, most, from_left, from_right, plus, minus):
    groups = total.shape[1] // LANES
    x = at[0]
    right, left = around(x, 1), around(x, -1)
    for message, came, owner in ((plus, from_left, right), (minus, from_right, RING + left)):
        start = rows_of(owner)
        head = head_of(came)
        unit = unit_of(most[...] + head * SPAN)
        write_head(message, unit)
        wide = lanes_of(head, STEP)
        fill(
            message,
            0,
            groups,
            gain_of(unit),
            lambda row, g, start=start, came=came, wide=wide: tile(total, start, row, g)
            + decode(block_at(came, 0, groups, g, row), wide),
        )


def gather_ring(at, total, left1, right1, left2, right2, both):
    groups = total.shape[1] // LANES
    x = at[0]
    for half, one, two in ((0, right1, left2), (1, left1, right2)):
        start = rows_of(half * RING + x)
        wide1, wide2 = lanes_of(head_of(one), STEP), lanes_of(head_of(two), STEP)

        def body(i, carry, half=half, one=one, two=two, start=start, wide1=wide1, wide2=wide2):
            row = pl.multiple_of(i * STEP, STEP)
            for g in range(groups):
                both[pl.ds(half * BLK + row, STEP), pl.ds(g * LANES, LANES)] = (
                    tile(total, start, row, g)
                    + decode(block_at(one, 1, groups, g, row), wide1)
                    + decode(block_at(two, 0, groups, g, row), wide2)
                )
            return carry

        lax.fori_loop(0, BLK // STEP, body, 0)


def send_rows(both, start, message):
    groups = both.shape[1] // LANES
    unit = unit_of(largest(both, start, BLK, groups))
    write_head(message, unit)
    fill(message, 0, groups, gain_of(unit), lambda row, g: tile(both, start, row, g))


def third_kernel(at, total, left1, right1, left2, right2, kept, message, both):
    gather_ring(at, total, left1, right1, left2, right2, both)
    half = at[1]
    send_rows(both, rows_of(1 - half), message)
    kept[...] = both[pl.ds(rows_of(half), BLK), :]


def same_kernel(at, before, kept, same):
    @pl.when(at[2] == 0)
    def _():
        send_rows(kept, 0, same)

    @pl.when(at[2] != 0)
    def _():
        send_rows(before, 0, same)


def add_up(out, kept, message, scale):
    groups = out.shape[1] // LANES
    plain = kept.dtype == jnp.float32
    wide = lanes_of(head_of(message), STEP)
    wide_kept = None if plain else lanes_of(head_of(kept), STEP)

    def body(i, carry):
        row = pl.multiple_of(i * STEP, STEP)
        for g in range(groups):
            if plain:
                mine = tile(kept, 0, row, g)
            else:
                mine = decode(block_at(kept, 0, groups, g, row), wide_kept)
            value = (mine + decode(block_at(message, 0, groups, g, row), wide)) * scale
            out[pl.ds(row, STEP), pl.ds(g * LANES, LANES)] = value
        return carry

    lax.fori_loop(0, BLK // STEP, body, 0)


def last_kernel(scale, kept, message, out):
    add_up(out, kept, message, scale[0])


def last_kernel_cross(scale, at, kept1, other1, kept2, other2, same, act, grad):
    @pl.when(at[0] == 0)
    def _():
        add_up(act, kept1, other1, scale[0])
        add_up(grad, same, other2, scale[0])

    @pl.when(at[0] != 0)
    def _():
        add_up(act, kept2, other2, scale[0])
        add_up(grad, same, other1, scale[0])


def call(kernel, ins, outs, scratch=(), scalars=1):
    return pl.pallas_call(
        kernel,
        out_shape=outs,
        in_specs=[SMEM] * scalars + [VMEM] * (len(ins) - scalars),
        out_specs=[VMEM] * len(outs),
        scratch_shapes=list(scratch),
        compiler_params=pltpu.CompilerParams(vmem_limit_bytes=LIMIT),
    )(*ins)


LIMIT = 20 * 2**20


def message_shape(pieces, width):
    return jax.ShapeDtypeStruct((HEAD + pieces * width, LANES), jnp.bfloat16)


def inner_tokens(left, right):
    return lax.dot_general(
        left, right, (((0,), (0,)), ((), ())), preferred_element_type=jnp.float32
    )


def statistics(acts, grads):
    width = acts.shape[1]
    per_layer = D // width
    shards = lax.axis_size("dp")
    spots = lax.axis_size("layer")
    f32 = jnp.float32
    place = lax.axis_index("dp")
    spot = lax.axis_index("layer")
    core = lax.rem(spot, 2)
    at = jnp.stack([lax.rem(place, RING), lax.div(place, RING), core]).astype(jnp.int32)
    scale = f32(1.0 / (acts.shape[0] * shards))
    plain_scale = jnp.full((1,), scale, f32)
    cross_scale = jnp.where(spot >= spots - per_layer, f32(0), scale).reshape(1)
    even = core == 0

    ring = [
        [(z * RING + x, z * RING + (x + by) % RING) for z in range(shards // RING) for x in range(RING)]
        for by in (1, -1)
    ]
    flip = [(d, (d + RING) % shards) for d in range(shards)]
    down = [(l, l - per_layer) for l in range(per_layer, spots)]

    def moves(parity, by):
        return [
            (l, l + by * per_layer)
            for l in range(spots)
            if l % 2 == parity and 0 <= l + by * per_layer < spots
        ]

    def across(parity):
        for l in range(spots):
            to = l if l % 2 == parity else l - per_layer
            if 0 <= to:
                for d in range(shards):
                    yield (l * shards + d, to * shards + (d + RING) % shards)

    def first(total):
        cols = total.shape[1]
        plus, minus, most = call(
            first_kernel, (at, total),
            (message_shape(2, cols), message_shape(2, cols), jax.ShapeDtypeStruct((8, LANES), f32)),
        )
        return (
            total, most,
            lax.ppermute(plus, "dp", ring[0]),
            lax.ppermute(minus, "dp", ring[1]),
        )

    def second(state):
        total, most, left1, right1 = state
        cols = total.shape[1]
        plus, minus = call(
            second_kernel, (at, total, most, left1, right1),
            (message_shape(1, cols), message_shape(1, cols)),
        )
        return (
            total, left1, right1,
            lax.ppermute(plus, "dp", ring[0]),
            lax.ppermute(minus, "dp", ring[1]),
        )

    def third(state):
        cols = state[0].shape[1]
        outs = (jax.ShapeDtypeStruct((BLK, cols), f32), message_shape(1, cols))
        scratch = (pltpu.VMEM((2 * BLK, cols), f32),)
        return call(third_kernel, (at,) + state, outs, scratch)

    acts_in = lax.ppermute(acts, "layer", moves(0, -1))
    grads_in = lax.ppermute(grads, "layer", moves(1, 1))
    u1 = first(inner_tokens(acts, acts))
    u2 = first(inner_tokens(grads, grads))
    u1 = second(u1)
    grads_in_later = lax.ppermute(grads, "layer", moves(0, 1))
    acts_in_later = lax.ppermute(acts, "layer", moves(1, -1))
    v1 = inner_tokens(jnp.where(even, acts, grads_in), jnp.where(even, acts_in, grads))
    v1 = first(v1)
    u2 = second(u2)
    kept_u1, out_u1 = third(u1)
    in_u1 = lax.ppermute(out_u1, "dp", flip)
    v1 = second(v1)
    v2 = inner_tokens(jnp.where(even, grads_in_later, acts), jnp.where(even, grads, acts_in_later))
    v2 = first(v2)
    kept_u2, out_u2 = third(u2)
    in_u2 = lax.ppermute(out_u2, "dp", flip)
    v2 = second(v2)
    kept_v1, out_v1 = third(v1)
    in_v1 = lax.ppermute(out_v1, ("layer", "dp"), list(across(0)))
    kept_v2, out_v2 = third(v2)
    in_v2 = lax.ppermute(out_v2, ("layer", "dp"), list(across(1)))
    same = call(same_kernel, (at, kept_v1, kept_v2), (message_shape(1, width),))[0]
    same_in = lax.ppermute(same, "layer", down)

    out_shape = jax.ShapeDtypeStruct((BLK, width), f32)
    act_diag = call(last_kernel, (plain_scale, kept_u1, in_u1), (out_shape,))[0]
    grad_diag = call(last_kernel, (plain_scale, kept_u2, in_u2), (out_shape,))[0]
    act_cross, grad_cross = call(
        last_kernel_cross,
        (cross_scale, core.reshape(1).astype(jnp.int32), kept_v1, in_v1, kept_v2, in_v2, same_in),
        (out_shape,) * 2, scalars=2,
    )
    return (act_diag, grad_diag, act_cross, grad_cross)


def solution(mesh):
    spec = P("dp", "layer")
    return jax.shard_map(
        statistics, mesh=mesh, in_specs=(spec,) * 2, out_specs=(spec,) * 4, check_vma=False
    )
```

profile of v0, /device:TPU:14, one launch (start us, length us, event | category | flops | bytes accessed | tf_op | source)
XLA Modules:
  0.0 160.0 jit_solution(5845414727326660310)
XLA Ops:
  0.6 3.5 %collective-permute-start.17 = (bf16[1024,1024]{1,0:T(8,128)(2,1)}, bf16[1024,1024]{1,0:T(8,128)(2,1)}, u32[]{:S(2)}, u32[]{:S(2)}) collective-permute-start(bf16[1024,1024]{1,0:T(8,128)(2,1)} %param.3), channel_id=1, source_target_pairs={{0,64},{16,80},{32,96},{48,112},{64,128},{80,144},{96,160},{112,17... | collective-permute-start | bytes 6291464 | tf_op jit(solution)/shard_map/ppermute | solution.py:320
  4.1 2.0 %collective-permute-start.18 = (bf16[1024,1024]{1,0:T(8,128)(2,1)}, bf16[1024,1024]{1,0:T(8,128)(2,1)}, u32[]{:S(2)}, u32[]{:S(2)}) collective-permute-start(bf16[1024,1024]{1,0:T(8,128)(2,1)} %param.2), channel_id=1, source_target_pairs={{72,8},{88,24},{104,40},{120,56},{136,72},{152,88},{168,104},{184,... | collective-permute-start | bytes 6291464 | tf_op jit(solution)/shard_map/ppermute | solution.py:321
  6.2 2.1 %collective-permute-start.10 = (bf16[1024,1024]{1,0:T(8,128)(2,1)}, bf16[1024,1024]{1,0:T(8,128)(2,1)}, u32[]{:S(2)}, u32[]{:S(2)}) collective-permute-start(bf16[1024,1024]{1,0:T(8,128)(2,1)} %param.3), channel_id=1, source_target_pairs={{8,72},{24,88},{40,104},{56,120},{72,136},{88,152},{104,168},{120,... | collective-permute-start | bytes 6291464 | tf_op jit(solution)/shard_map/ppermute | solution.py:316
  8.2 3.7 %collective-permute-start.11 = (bf16[1024,1024]{1,0:T(8,128)(2,1)}, bf16[1024,1024]{1,0:T(8,128)(2,1)}, u32[]{:S(2)}, u32[]{:S(2)}) collective-permute-start(bf16[1024,1024]{1,0:T(8,128)(2,1)} %param.2), channel_id=1, source_target_pairs={{64,0},{80,16},{96,32},{112,48},{128,64},{144,80},{160,96},{176,11... | collective-permute-start | bytes 6291464 | tf_op jit(solution)/shard_map/ppermute | solution.py:315
  12.0 0.1 pad_add_fusion.at
  12.0 4.7 %fusion.9.total = f32[1024,1024]{1,0:T(8,128)S(1)} fusion(bf16[1024,1024]{1,0:T(8,128)(2,1)} %param.3), kind=kOutput, calls=%fused_computation.10 | convolution fusion | flops 2147483648 | bytes 6291456 | tf_op jit(solution)/shard_map/dot_general | solution.py:243
  16.7 0.0 copy-start.2
  16.7 3.5 %shard_map.61 = (bf16[2064,128]{1,0:T(8,128)(2,1)}, bf16[2064,128]{1,0:T(8,128)(2,1)S(1)}, f32[8,128]{1,0:T(8,128)S(1)}) custom-call(s32[3]{0:T(128)S(1)} %pad_add_fusion.at, f32[1024,1024]{1,0:T(8,128)S(1)} %fusion.9.total), custom_call_target="tpu_custom_call" | custom-call | tf_op jit(solution)/shard_map/pallas_call | solution.py:225
  20.2 0.5 collective-permute-start.5
  20.7 2.4 %fusion.8.total = f32[1024,1024]{1,0:T(8,128)S(1)} fusion(bf16[1024,1024]{1,0:T(8,128)(2,1)S(1)} %copy-done.2), kind=kOutput, calls=%fused_computation.9 | convolution fusion | flops 2147483648 | bytes 6291456 | tf_op jit(solution)/shard_map/dot_general | solution.py:243
  23.1 0.0 copy-start.3
  23.1 0.0 copy-start.4
  23.1 2.7 %shard_map.57 = (bf16[2064,128]{1,0:T(8,128)(2,1)S(1)}, bf16[2064,128]{1,0:T(8,128)(2,1)S(1)}, f32[8,128]{1,0:T(8,128)S(1)}) custom-call(s32[3]{0:T(128)S(1)} %pad_add_fusion.at, f32[1024,1024]{1,0:T(8,128)S(1)} %fusion.8.total), custom_call_target="tpu_custom_call" | custom-call | tf_op jit(solution)/shard_map/pallas_call | solution.py:225
  25.8 22.6 %collective-permute-done.17 = bf16[1024,1024]{1,0:T(8,128)(2,1)} collective-permute-done((bf16[1024,1024]{1,0:T(8,128)(2,1)}, bf16[1024,1024]{1,0:T(8,128)(2,1)}, u32[]{:S(2)}, u32[]{:S(2)}) %collective-permute-start.17) | collective-permute-done | bytes 2097184 | tf_op jit(solution)/shard_map/ppermute | solution.py:320
  48.3 0.8 collective-permute-start.6
  49.2 0.0 collective-permute-done.18
  49.2 2.4 %collective-permute-start = (bf16[2064,128]{1,0:T(8,128)(2,1)S(1)}, bf16[2064,128]{1,0:T(8,128)(2,1)S(1)}, u32[]{:S(2)}, u32[]{:S(2)}) collective-permute-start(bf16[2064,128]{1,0:T(8,128)(2,1)S(1)} %get-tuple-element.34), channel_id=1, source_target_pairs={{0,1},{1,2},{2,3},{3,0},{4,5},{5,6},{6,7},{7,4},{8,9},{9,10},{10,1... | collective-permute-start | bytes 1585160 | tf_op jit(solution)/shard_map/ppermute | solution.py:292
  51.6 4.1 %fusion.total = f32[1024,1024]{1,0:T(8,128)S(1)} fusion(bf16[1024,1024]{1,0:T(8,128)(2,1)S(1)} %copy-done.4, bf16[1024,1024]{1,0:T(8,128)(2,1)} %collective-permute-done.18, bf16[1024,1024]{1,0:T(8,128)(2,1)} %collective-permute-done.17, bf16[1024,1024]{1,0:T(8,128)(2,1)S(1)} %copy-done.3, pred[]{:T(512)S(6)} %eq.3), kind=kOutput, calls=%fused_computation | convolution fusion | flops 2149580800 | bytes 12582913 | tf_op jit(solution)/shard_map/dot_general | solution.py:243
  55.7 2.7 %shard_map.68 = (bf16[2064,128]{1,0:T(8,128)(2,1)S(1)}, bf16[2064,128]{1,0:T(8,128)(2,1)S(1)}, f32[8,128]{1,0:T(8,128)S(1)}) custom-call(s32[3]{0:T(128)S(1)} %pad_add_fusion.at, f32[1024,1024]{1,0:T(8,128)S(1)} %fusion.total), custom_call_target="tpu_custom_call" | custom-call | tf_op jit(solution)/shard_map/pallas_call | solution.py:225
  58.4 0.0 collective-permute-done.5.from_left.left1
  58.4 0.1 collective-permute-start.1
  58.5 0.0 collective-permute-done.10
  58.5 3.2 %collective-permute-start.19 = (bf16[2064,128]{1,0:T(8,128)(2,1)S(1)}, bf16[2064,128]{1,0:T(8,128)(2,1)S(1)}, u32[]{:S(2)}, u32[]{:S(2)}) collective-permute-start(bf16[2064,128]{1,0:T(8,128)(2,1)S(1)} %get-tuple-element.55), channel_id=1, source_target_pairs={{0,1},{1,2},{2,3},{3,0},{4,5},{5,6},{6,7},{7,4},{8,9},{9,10},{10,1... | collective-permute-start | bytes 1585160 | tf_op jit(solution)/shard_map/ppermute | solution.py:292
  61.7 0.0 collective-permute-done.11
  61.7 0.0 collective-permute-start.20
  61.7 4.1 %fusion.3.total = f32[1024,1024]{1,0:T(8,128)S(1)} fusion(bf16[1024,1024]{1,0:T(8,128)(2,1)} %collective-permute-done.11, bf16[1024,1024]{1,0:T(8,128)(2,1)S(1)} %copy-done.4, bf16[1024,1024]{1,0:T(8,128)(2,1)S(1)} %copy-done.3, bf16[1024,1024]{1,0:T(8,128)(2,1)} %collective-permute-done.10, pred[]{:T(512)S(6)} %eq.3), kind=kOutput, calls=%fused_computation.3 | convolution fusion | flops 2149580800 | bytes 12582913 | tf_op jit(solution)/shard_map/dot_general | solution.py:243
  65.8 2.7 %shard_map.65 = (bf16[2064,128]{1,0:T(8,128)(2,1)S(1)}, bf16[2064,128]{1,0:T(8,128)(2,1)S(1)}, f32[8,128]{1,0:T(8,128)S(1)}) custom-call(s32[3]{0:T(128)S(1)} %pad_add_fusion.at, f32[1024,1024]{1,0:T(8,128)S(1)} %fusion.3.total), custom_call_target="tpu_custom_call" | custom-call | tf_op jit(solution)/shard_map/pallas_call | solution.py:225
  68.5 0.0 collective-permute-done.6.from_right.right1
  68.5 3.3 %collective-permute-start.12 = (bf16[2064,128]{1,0:T(8,128)(2,1)S(1)}, bf16[2064,128]{1,0:T(8,128)(2,1)S(1)}, u32[]{:S(2)}, u32[]{:S(2)}) collective-permute-start(bf16[2064,128]{1,0:T(8,128)(2,1)S(1)} %get-tuple-element.48), channel_id=1, source_target_pairs={{0,1},{1,2},{2,3},{3,0},{4,5},{5,6},{6,7},{7,4},{8,9},{9,10},{10,1... | collective-permute-start | bytes 1585160 | tf_op jit(solution)/shard_map/ppermute | solution.py:292
  71.8 0.0 collective-permute-done.from_left.left1
  71.8 0.0 collective-permute-start.13
  71.8 1.5 shard_map.62
  73.3 1.2 collective-permute-done.1.from_right.right1
  74.5 2.1 %collective-permute-start.7 = (bf16[1040,128]{1,0:T(8,128)(2,1)S(1)}, bf16[1040,128]{1,0:T(8,128)(2,1)S(1)}, u32[]{:S(2)}, u32[]{:S(2)}) collective-permute-start(bf16[1040,128]{1,0:T(8,128)(2,1)S(1)} %get-tuple-element.44), channel_id=1, source_target_pairs={{0,1},{1,2},{2,3},{3,0},{4,5},{5,6},{6,7},{7,4},{8,9},{9,10},{10,1... | collective-permute-start | bytes 798728 | tf_op jit(solution)/shard_map/ppermute | solution.py:305
  76.6 1.5 shard_map.58
  78.2 0.0 collective-permute-done.19.from_left.left1
  78.2 0.1 collective-permute-start.8
  78.3 7.6 %collective-permute-done.20.from_right.right1 = bf16[2064,128]{1,0:T(8,128)(2,1)S(1)} collective-permute-done((bf16[2064,128]{1,0:T(8,128)(2,1)S(1)}, bf16[2064,128]{1,0:T(8,128)(2,1)S(1)}, u32[]{:S(2)}, u32[]{:S(2)}) %collective-permute-start.20) | collective-permute-done | bytes 528416 | tf_op jit(solution)/shard_map/ppermute | solution.py:293
  85.9 0.0 collective-permute-start.2
  85.9 1.5 shard_map.69
  87.4 0.0 collective-permute-done.12.from_left.left1
  87.4 2.1 %collective-permute-start.3 = (bf16[1040,128]{1,0:T(8,128)(2,1)S(1)}, bf16[1040,128]{1,0:T(8,128)(2,1)S(1)}, u32[]{:S(2)}, u32[]{:S(2)}) collective-permute-start(bf16[1040,128]{1,0:T(8,128)(2,1)S(1)} %get-tuple-element.38), channel_id=1, source_target_pairs={{0,3},{1,0},{2,1},{3,2},{4,7},{5,4},{6,5},{7,6},{8,11},{9,8},{10,9... | collective-permute-start | bytes 798728 | tf_op jit(solution)/shard_map/ppermute | solution.py:306
  89.5 7.7 %collective-permute-done.13.from_right.right1 = bf16[2064,128]{1,0:T(8,128)(2,1)S(1)} collective-permute-done((bf16[2064,128]{1,0:T(8,128)(2,1)S(1)}, bf16[2064,128]{1,0:T(8,128)(2,1)S(1)}, u32[]{:S(2)}, u32[]{:S(2)}) %collective-permute-start.13) | collective-permute-done | bytes 528416 | tf_op jit(solution)/shard_map/ppermute | solution.py:293
  97.2 1.5 shard_map.66
  98.7 2.1 %collective-permute-start.22 = (bf16[1040,128]{1,0:T(8,128)(2,1)S(1)}, bf16[1040,128]{1,0:T(8,128)(2,1)S(1)}, u32[]{:S(2)}, u32[]{:S(2)}) collective-permute-start(bf16[1040,128]{1,0:T(8,128)(2,1)S(1)} %get-tuple-element.59), channel_id=1, source_target_pairs={{0,3},{1,0},{2,1},{3,2},{4,7},{5,4},{6,5},{7,6},{8,11},{9,8},{10,9... | collective-permute-start | bytes 798728 | tf_op jit(solution)/shard_map/ppermute | solution.py:306
  100.8 2.1 %collective-permute-done.8.right2 = bf16[1040,128]{1,0:T(8,128)(2,1)S(1)} collective-permute-done((bf16[1040,128]{1,0:T(8,128)(2,1)S(1)}, bf16[1040,128]{1,0:T(8,128)(2,1)S(1)}, u32[]{:S(2)}, u32[]{:S(2)}) %collective-permute-start.8) | collective-permute-done | bytes 266272 | tf_op jit(solution)/shard_map/ppermute | solution.py:306
  102.9 2.0 %collective-permute-start.15 = (bf16[1040,128]{1,0:T(8,128)(2,1)S(1)}, bf16[1040,128]{1,0:T(8,128)(2,1)S(1)}, u32[]{:S(2)}, u32[]{:S(2)}) collective-permute-start(bf16[1040,128]{1,0:T(8,128)(2,1)S(1)} %get-tuple-element.52), channel_id=1, source_target_pairs={{0,3},{1,0},{2,1},{3,2},{4,7},{5,4},{6,5},{7,6},{8,11},{9,8},{10,9... | collective-permute-start | bytes 798728 | tf_op jit(solution)/shard_map/ppermute | solution.py:306
  104.9 2.7 %shard_map.63 = (f32[128,1024]{1,0:T(8,128)S(1)}, bf16[1040,128]{1,0:T(8,128)(2,1)}) custom-call(s32[3]{0:T(128)S(1)} %pad_add_fusion.at, f32[1024,1024]{1,0:T(8,128)S(1)} %copy-done.1, bf16[2064,128]{1,0:T(8,128)(2,1)S(1)} %collective-permute-done.5.from_left.left1, bf16[2064,128]{1,0:T(8,128)(2,1)S(1)} %collective-permute-done.6.from_right.right1, ...), custom_call_target="tpu_custom_call" | custom-call | tf_op jit(solution)/shard_map/pallas_call | solution.py:225
  107.7 0.9 collective-permute-done.3.right2
  108.6 7.2 %collective-permute-start.9 = (bf16[1040,128]{1,0:T(8,128)(2,1)}, bf16[1040,128]{1,0:T(8,128)(2,1)S(1)}, u32[]{:S(2)}, u32[]{:S(2)}) collective-permute-start(bf16[1040,128]{1,0:T(8,128)(2,1)} %get-tuple-element.47), channel_id=1, source_target_pairs={{0,4},{1,5},{2,6},{3,7},{4,0},{5,1},{6,2},{7,3},{8,12},{9,13},{10,... | collective-permute-start | bytes 798728 | tf_op jit(solution)/shard_map/ppermute | solution.py:331
  115.8 2.7 %shard_map.59 = (f32[128,1024]{1,0:T(8,128)S(1)}, bf16[1040,128]{1,0:T(8,128)(2,1)}) custom-call(s32[3]{0:T(128)S(1)} %pad_add_fusion.at, f32[1024,1024]{1,0:T(8,128)S(1)} %fusion.8.total, bf16[2064,128]{1,0:T(8,128)(2,1)S(1)} %collective-permute-done.from_left.left1, bf16[2064,128]{1,0:T(8,128)(2,1)S(1)} %collective-permute-done.1.from_right.right1, ...), custom_call_target="tpu_custom_call" | custom-call | tf_op jit(solution)/shard_map/pallas_call | solution.py:225
  118.5 0.0 collective-permute-start.4
  118.5 2.7 %shard_map.70 = (f32[128,1024]{1,0:T(8,128)S(1)}, bf16[1040,128]{1,0:T(8,128)(2,1)}) custom-call(s32[3]{0:T(128)S(1)} %pad_add_fusion.at, f32[1024,1024]{1,0:T(8,128)S(1)} %fusion.total, bf16[2064,128]{1,0:T(8,128)(2,1)S(1)} %collective-permute-done.19.from_left.left1, bf16[2064,128]{1,0:T(8,128)(2,1)S(1)} %collective-permute-done.20.from_right.right1, ...), custom_call_target="tpu_custom_call" | custom-call | tf_op jit(solution)/shard_map/pallas_call | solution.py:225
  121.3 2.7 %shard_map.67 = (f32[128,1024]{1,0:T(8,128)S(1)}, bf16[1040,128]{1,0:T(8,128)(2,1)}) custom-call(s32[3]{0:T(128)S(1)} %pad_add_fusion.at, f32[1024,1024]{1,0:T(8,128)S(1)} %fusion.3.total, bf16[2064,128]{1,0:T(8,128)(2,1)S(1)} %collective-permute-done.12.from_left.left1, bf16[2064,128]{1,0:T(8,128)(2,1)S(1)} %collective-permute-done.13.from_right.right1, ...), custom_call_target="tpu_custom_call" | custom-call | tf_op jit(solution)/shard_map/pallas_call | solution.py:225
  124.0 1.7 %shard_map.71 = bf16[1040,128]{1,0:T(8,128)(2,1)} custom-call(s32[3]{0:T(128)S(1)} %pad_add_fusion.at, f32[128,1024]{1,0:T(8,128)S(1)} %get-tuple-element.53.before.kept1, f32[128,1024]{1,0:T(8,128)S(1)} %get-tuple-element.60.kept.kept2), custom_call_target="tpu_custom_call" | custom-call | tf_op jit(solution)/shard_map/pallas_call | solution.py:225
  125.8 1.9 %collective-permute-start.24 = (bf16[1040,128]{1,0:T(8,128)(2,1)}, bf16[1040,128]{1,0:T(8,128)(2,1)S(1)}, u32[]{:S(2)}, u32[]{:S(2)}) collective-permute-start(bf16[1040,128]{1,0:T(8,128)(2,1)} %shard_map.71), channel_id=1, source_target_pairs={{64,0},{72,8},{80,16},{88,24},{96,32},{104,40},{112,48},{120,56},{... | collective-permute-start | bytes 798728 | tf_op jit(solution)/shard_map/ppermute | solution.py:338
  127.7 6.2 %collective-permute-start.23 = (bf16[1040,128]{1,0:T(8,128)(2,1)}, bf16[1040,128]{1,0:T(8,128)(2,1)S(1)}, u32[]{:S(2)}, u32[]{:S(2)}) collective-permute-start(bf16[1040,128]{1,0:T(8,128)(2,1)} %get-tuple-element.61), channel_id=1, source_target_pairs={{8,12},{9,13},{10,14},{11,15},{12,8},{13,9},{14,10},{15,11},{24,28... | collective-permute-start | bytes 798728 | tf_op jit(solution)/shard_map/ppermute | solution.py:336
  133.9 3.6 %collective-permute-start.16 = (bf16[1040,128]{1,0:T(8,128)(2,1)}, bf16[1040,128]{1,0:T(8,128)(2,1)S(1)}, u32[]{:S(2)}, u32[]{:S(2)}) collective-permute-start(bf16[1040,128]{1,0:T(8,128)(2,1)} %get-tuple-element.54), channel_id=1, source_target_pairs={{0,4},{1,5},{2,6},{3,7},{4,0},{5,1},{6,2},{7,3},{16,20},{17,21},{1... | collective-permute-start | bytes 798728 | tf_op jit(solution)/shard_map/ppermute | solution.py:334
  137.5 1.1 shard_map.64
  138.6 6.4 %collective-permute-done.4.message = bf16[1040,128]{1,0:T(8,128)(2,1)S(1)} collective-permute-done((bf16[1040,128]{1,0:T(8,128)(2,1)}, bf16[1040,128]{1,0:T(8,128)(2,1)S(1)}, u32[]{:S(2)}, u32[]{:S(2)}) %collective-permute-start.4) | collective-permute-done | bytes 266272 | tf_op jit(solution)/shard_map/ppermute | solution.py:326
  145.0 1.1 shard_map.60
  146.1 10.2 %collective-permute-done.23.other2 = bf16[1040,128]{1,0:T(8,128)(2,1)S(1)} collective-permute-done((bf16[1040,128]{1,0:T(8,128)(2,1)}, bf16[1040,128]{1,0:T(8,128)(2,1)S(1)}, u32[]{:S(2)}, u32[]{:S(2)}) %collective-permute-start.23) | collective-permute-done | bytes 266272 | tf_op jit(solution)/shard_map/ppermute | solution.py:336
  156.2 1.9 %collective-permute-done.16.other1 = bf16[1040,128]{1,0:T(8,128)(2,1)S(1)} collective-permute-done((bf16[1040,128]{1,0:T(8,128)(2,1)}, bf16[1040,128]{1,0:T(8,128)(2,1)S(1)}, u32[]{:S(2)}, u32[]{:S(2)}) %collective-permute-start.16) | collective-permute-done | bytes 266272 | tf_op jit(solution)/shard_map/ppermute | solution.py:334
  158.2 1.8 %shard_map.72 = (f32[128,1024]{1,0:T(8,128)}, f32[128,1024]{1,0:T(8,128)}) custom-call(f32[1]{0:T(128)} %bitcast.3.scale, s32[1]{0:T(128)} %bitcast.2.at, f32[128,1024]{1,0:T(8,128)S(1)} %get-tuple-element.53.before.kept1, bf16[1040,128]{1,0:T(8,128)(2,1)S(1)} %collective-permute-done.16.other1, f32[128,1024]{1,0:T(8,128)S(1)} %get-tuple-element.60.kept.kept2, ...), custom_call_target="tpu_custom_call" | custom-call | tf_op jit(solution)/shard_map/pallas_call | solution.py:225
  (17 shorter events, 0.0 us)
Async XLA Ops:
  0.6 47.7 %collective-permute-start.17 = (bf16[1024,1024]{1,0:T(8,128)(2,1)}, bf16[1024,1024]{1,0:T(8,128)(2,1)}, u32[]{:S(2)}, u32[]{:S(2)}) collective-permute-start(bf16[1024,1024]{1,0:T(8,128)(2,1)} %param.3), channel_id=1, source_target_pairs={{0,64},{16,80},{32,96},{48,112},{64,128},{80,144},{96,160},{112,17... | collective-permute-start | bytes 6291464 | tf_op jit(solution)/shard_map/ppermute | solution.py:320
  4.1 45.1 %collective-permute-start.18 = (bf16[1024,1024]{1,0:T(8,128)(2,1)}, bf16[1024,1024]{1,0:T(8,128)(2,1)}, u32[]{:S(2)}, u32[]{:S(2)}) collective-permute-start(bf16[1024,1024]{1,0:T(8,128)(2,1)} %param.2), channel_id=1, source_target_pairs={{72,8},{88,24},{104,40},{120,56},{136,72},{152,88},{168,104},{184,... | collective-permute-start | bytes 6291464 | tf_op jit(solution)/shard_map/ppermute | solution.py:321
  6.2 52.3 %collective-permute-start.10 = (bf16[1024,1024]{1,0:T(8,128)(2,1)}, bf16[1024,1024]{1,0:T(8,128)(2,1)}, u32[]{:S(2)}, u32[]{:S(2)}) collective-permute-start(bf16[1024,1024]{1,0:T(8,128)(2,1)} %param.3), channel_id=1, source_target_pairs={{8,72},{24,88},{40,104},{56,120},{72,136},{88,152},{104,168},{120,... | collective-permute-start | bytes 6291464 | tf_op jit(solution)/shard_map/ppermute | solution.py:316
  8.2 53.5 %collective-permute-start.11 = (bf16[1024,1024]{1,0:T(8,128)(2,1)}, bf16[1024,1024]{1,0:T(8,128)(2,1)}, u32[]{:S(2)}, u32[]{:S(2)}) collective-permute-start(bf16[1024,1024]{1,0:T(8,128)(2,1)} %param.2), channel_id=1, source_target_pairs={{64,0},{80,16},{96,32},{112,48},{128,64},{144,80},{160,96},{176,11... | collective-permute-start | bytes 6291464 | tf_op jit(solution)/shard_map/ppermute | solution.py:315
  16.7 3.5 %copy-start = (f32[1024,1024]{1,0:T(8,128)}, f32[1024,1024]{1,0:T(8,128)S(1)}, u32[]{:S(2)}) copy-start(f32[1024,1024]{1,0:T(8,128)S(1)} %fusion.9.total) | copy-start | bytes 12582916
  16.7 4.0 %copy-start.2 = (bf16[1024,1024]{1,0:T(8,128)(2,1)S(1)}, bf16[1024,1024]{1,0:T(8,128)(2,1)}, u32[]{:S(2)}) copy-start(bf16[1024,1024]{1,0:T(8,128)(2,1)} %param.2) | copy-start | bytes 6291460
  20.2 38.2 %collective-permute-start.5 = (bf16[2064,128]{1,0:T(8,128)(2,1)}, bf16[2064,128]{1,0:T(8,128)(2,1)S(1)}, u32[]{:S(2)}, u32[]{:S(2)}) collective-permute-start(bf16[2064,128]{1,0:T(8,128)(2,1)} %get-tuple-element.41), channel_id=1, source_target_pairs={{0,1},{1,2},{2,3},{3,0},{4,5},{5,6},{6,7},{7,4},{8,9},{9,10},{10,1... | collective-permute-start | bytes 1585160 | tf_op jit(solution)/shard_map/ppermute | solution.py:292
  23.1 28.5 %copy-start.3 = (bf16[1024,1024]{1,0:T(8,128)(2,1)S(1)}, bf16[1024,1024]{1,0:T(8,128)(2,1)}, u32[]{:S(2)}) copy-start(bf16[1024,1024]{1,0:T(8,128)(2,1)} %param.2) | copy-start | bytes 6291460
  23.1 28.5 %copy-start.4 = (bf16[1024,1024]{1,0:T(8,128)(2,1)S(1)}, bf16[1024,1024]{1,0:T(8,128)(2,1)}, u32[]{:S(2)}) copy-start(bf16[1024,1024]{1,0:T(8,128)(2,1)} %param.3) | copy-start | bytes 6291460
  48.3 20.1 %collective-permute-start.6 = (bf16[2064,128]{1,0:T(8,128)(2,1)S(1)}, bf16[2064,128]{1,0:T(8,128)(2,1)S(1)}, u32[]{:S(2)}, u32[]{:S(2)}) collective-permute-start(bf16[2064,128]{1,0:T(8,128)(2,1)S(1)} %get-tuple-element.42), channel_id=1, source_target_pairs={{0,3},{1,0},{2,1},{3,2},{4,7},{5,4},{6,5},{7,6},{8,11},{9,8},{10,9... | collective-permute-start | bytes 1585160 | tf_op jit(solution)/shard_map/ppermute | solution.py:293
  49.2 22.6 %collective-permute-start = (bf16[2064,128]{1,0:T(8,128)(2,1)S(1)}, bf16[2064,128]{1,0:T(8,128)(2,1)S(1)}, u32[]{:S(2)}, u32[]{:S(2)}) collective-permute-start(bf16[2064,128]{1,0:T(8,128)(2,1)S(1)} %get-tuple-element.34), channel_id=1, source_target_pairs={{0,1},{1,2},{2,3},{3,0},{4,5},{5,6},{6,7},{7,4},{8,9},{9,10},{10,1... | collective-permute-start | bytes 1585160 | tf_op jit(solution)/shard_map/ppermute | solution.py:292
  58.4 16.2 %collective-permute-start.1 = (bf16[2064,128]{1,0:T(8,128)(2,1)S(1)}, bf16[2064,128]{1,0:T(8,128)(2,1)S(1)}, u32[]{:S(2)}, u32[]{:S(2)}) collective-permute-start(bf16[2064,128]{1,0:T(8,128)(2,1)S(1)} %get-tuple-element.35), channel_id=1, source_target_pairs={{0,3},{1,0},{2,1},{3,2},{4,7},{5,4},{6,5},{7,6},{8,11},{9,8},{10,9... | collective-permute-start | bytes 1585160 | tf_op jit(solution)/shard_map/ppermute | solution.py:293
  58.5 19.7 %collective-permute-start.19 = (bf16[2064,128]{1,0:T(8,128)(2,1)S(1)}, bf16[2064,128]{1,0:T(8,128)(2,1)S(1)}, u32[]{:S(2)}, u32[]{:S(2)}) collective-permute-start(bf16[2064,128]{1,0:T(8,128)(2,1)S(1)} %get-tuple-element.55), channel_id=1, source_target_pairs={{0,1},{1,2},{2,3},{3,0},{4,5},{5,6},{6,7},{7,4},{8,9},{9,10},{10,1... | collective-permute-start | bytes 1585160 | tf_op jit(solution)/shard_map/ppermute | solution.py:292
  61.7 24.2 %collective-permute-start.20 = (bf16[2064,128]{1,0:T(8,128)(2,1)S(1)}, bf16[2064,128]{1,0:T(8,128)(2,1)S(1)}, u32[]{:S(2)}, u32[]{:S(2)}) collective-permute-start(bf16[2064,128]{1,0:T(8,128)(2,1)S(1)} %get-tuple-element.56), channel_id=1, source_target_pairs={{0,3},{1,0},{2,1},{3,2},{4,7},{5,4},{6,5},{7,6},{8,11},{9,8},{10,9... | collective-permute-start | bytes 1585160 | tf_op jit(solution)/shard_map/ppermute | solution.py:293
  65.8 6.0 %copy-start.1 = (f32[1024,1024]{1,0:T(8,128)S(1)}, f32[1024,1024]{1,0:T(8,128)}, u32[]{:S(2)}) copy-start(f32[1024,1024]{1,0:T(8,128)} %copy-done) | copy-start | bytes 12582916
  68.5 18.9 %collective-permute-start.12 = (bf16[2064,128]{1,0:T(8,128)(2,1)S(1)}, bf16[2064,128]{1,0:T(8,128)(2,1)S(1)}, u32[]{:S(2)}, u32[]{:S(2)}) collective-permute-start(bf16[2064,128]{1,0:T(8,128)(2,1)S(1)} %get-tuple-element.48), channel_id=1, source_target_pairs={{0,1},{1,2},{2,3},{3,0},{4,5},{5,6},{6,7},{7,4},{8,9},{9,10},{10,1... | collective-permute-start | bytes 1585160 | tf_op jit(solution)/shard_map/ppermute | solution.py:292
  71.8 25.4 %collective-permute-start.13 = (bf16[2064,128]{1,0:T(8,128)(2,1)S(1)}, bf16[2064,128]{1,0:T(8,128)(2,1)S(1)}, u32[]{:S(2)}, u32[]{:S(2)}) collective-permute-start(bf16[2064,128]{1,0:T(8,128)(2,1)S(1)} %get-tuple-element.49), channel_id=1, source_target_pairs={{0,3},{1,0},{2,1},{3,2},{4,7},{5,4},{6,5},{7,6},{8,11},{9,8},{10,9... | collective-permute-start | bytes 1585160 | tf_op jit(solution)/shard_map/ppermute | solution.py:293
  74.5 24.2 %collective-permute-start.7 = (bf16[1040,128]{1,0:T(8,128)(2,1)S(1)}, bf16[1040,128]{1,0:T(8,128)(2,1)S(1)}, u32[]{:S(2)}, u32[]{:S(2)}) collective-permute-start(bf16[1040,128]{1,0:T(8,128)(2,1)S(1)} %get-tuple-element.44), channel_id=1, source_target_pairs={{0,1},{1,2},{2,3},{3,0},{4,5},{5,6},{6,7},{7,4},{8,9},{9,10},{10,1... | collective-permute-start | bytes 798728 | tf_op jit(solution)/shard_map/ppermute | solution.py:305
  78.2 24.7 %collective-permute-start.8 = (bf16[1040,128]{1,0:T(8,128)(2,1)S(1)}, bf16[1040,128]{1,0:T(8,128)(2,1)S(1)}, u32[]{:S(2)}, u32[]{:S(2)}) collective-permute-start(bf16[1040,128]{1,0:T(8,128)(2,1)S(1)} %get-tuple-element.45), channel_id=1, source_target_pairs={{0,3},{1,0},{2,1},{3,2},{4,7},{5,4},{6,5},{7,6},{8,11},{9,8},{10,9... | collective-permute-start | bytes 798728 | tf_op jit(solution)/shard_map/ppermute | solution.py:306
  85.9 17.0 %collective-permute-start.2 = (bf16[1040,128]{1,0:T(8,128)(2,1)S(1)}, bf16[1040,128]{1,0:T(8,128)(2,1)S(1)}, u32[]{:S(2)}, u32[]{:S(2)}) collective-permute-start(bf16[1040,128]{1,0:T(8,128)(2,1)S(1)} %get-tuple-element.37), channel_id=1, source_target_pairs={{0,1},{1,2},{2,3},{3,0},{4,5},{5,6},{6,7},{7,4},{8,9},{9,10},{10,1... | collective-permute-start | bytes 798728 | tf_op jit(solution)/shard_map/ppermute | solution.py:305
  87.4 21.2 %collective-permute-start.3 = (bf16[1040,128]{1,0:T(8,128)(2,1)S(1)}, bf16[1040,128]{1,0:T(8,128)(2,1)S(1)}, u32[]{:S(2)}, u32[]{:S(2)}) collective-permute-start(bf16[1040,128]{1,0:T(8,128)(2,1)S(1)} %get-tuple-element.38), channel_id=1, source_target_pairs={{0,3},{1,0},{2,1},{3,2},{4,7},{5,4},{6,5},{7,6},{8,11},{9,8},{10,9... | collective-permute-start | bytes 798728 | tf_op jit(solution)/shard_map/ppermute | solution.py:306
  97.2 21.3 %collective-permute-start.21 = (bf16[1040,128]{1,0:T(8,128)(2,1)S(1)}, bf16[1040,128]{1,0:T(8,128)(2,1)S(1)}, u32[]{:S(2)}, u32[]{:S(2)}) collective-permute-start(bf16[1040,128]{1,0:T(8,128)(2,1)S(1)} %get-tuple-element.58), channel_id=1, source_target_pairs={{0,1},{1,2},{2,3},{3,0},{4,5},{5,6},{6,7},{7,4},{8,9},{9,10},{10,1... | collective-permute-start | bytes 798728 | tf_op jit(solution)/shard_map/ppermute | solution.py:305
  98.7 19.8 %collective-permute-start.22 = (bf16[1040,128]{1,0:T(8,128)(2,1)S(1)}, bf16[1040,128]{1,0:T(8,128)(2,1)S(1)}, u32[]{:S(2)}, u32[]{:S(2)}) collective-permute-start(bf16[1040,128]{1,0:T(8,128)(2,1)S(1)} %get-tuple-element.59), channel_id=1, source_target_pairs={{0,3},{1,0},{2,1},{3,2},{4,7},{5,4},{6,5},{7,6},{8,11},{9,8},{10,9... | collective-permute-start | bytes 798728 | tf_op jit(solution)/shard_map/ppermute | solution.py:306
  102.9 18.4 %collective-permute-start.14 = (bf16[1040,128]{1,0:T(8,128)(2,1)S(1)}, bf16[1040,128]{1,0:T(8,128)(2,1)S(1)}, u32[]{:S(2)}, u32[]{:S(2)}) collective-permute-start(bf16[1040,128]{1,0:T(8,128)(2,1)S(1)} %get-tuple-element.51), channel_id=1, source_target_pairs={{0,1},{1,2},{2,3},{3,0},{4,5},{5,6},{6,7},{7,4},{8,9},{9,10},{10,1... | collective-permute-start | bytes 798728 | tf_op jit(solution)/shard_map/ppermute | solution.py:305
  102.9 18.4 %collective-permute-start.15 = (bf16[1040,128]{1,0:T(8,128)(2,1)S(1)}, bf16[1040,128]{1,0:T(8,128)(2,1)S(1)}, u32[]{:S(2)}, u32[]{:S(2)}) collective-permute-start(bf16[1040,128]{1,0:T(8,128)(2,1)S(1)} %get-tuple-element.52), channel_id=1, source_target_pairs={{0,3},{1,0},{2,1},{3,2},{4,7},{5,4},{6,5},{7,6},{8,11},{9,8},{10,9... | collective-permute-start | bytes 798728 | tf_op jit(solution)/shard_map/ppermute | solution.py:306
  108.6 28.8 %collective-permute-start.9 = (bf16[1040,128]{1,0:T(8,128)(2,1)}, bf16[1040,128]{1,0:T(8,128)(2,1)S(1)}, u32[]{:S(2)}, u32[]{:S(2)}) collective-permute-start(bf16[1040,128]{1,0:T(8,128)(2,1)} %get-tuple-element.47), channel_id=1, source_target_pairs={{0,4},{1,5},{2,6},{3,7},{4,0},{5,1},{6,2},{7,3},{8,12},{9,13},{10,... | collective-permute-start | bytes 798728 | tf_op jit(solution)/shard_map/ppermute | solution.py:331
  118.5 26.5 %collective-permute-start.4 = (bf16[1040,128]{1,0:T(8,128)(2,1)}, bf16[1040,128]{1,0:T(8,128)(2,1)S(1)}, u32[]{:S(2)}, u32[]{:S(2)}) collective-permute-start(bf16[1040,128]{1,0:T(8,128)(2,1)} %get-tuple-element.40), channel_id=1, source_target_pairs={{0,4},{1,5},{2,6},{3,7},{4,0},{5,1},{6,2},{7,3},{8,12},{9,13},{10,... | collective-permute-start | bytes 798728 | tf_op jit(solution)/shard_map/ppermute | solution.py:326
  125.8 20.3 %collective-permute-start.24 = (bf16[1040,128]{1,0:T(8,128)(2,1)}, bf16[1040,128]{1,0:T(8,128)(2,1)S(1)}, u32[]{:S(2)}, u32[]{:S(2)}) collective-permute-start(bf16[1040,128]{1,0:T(8,128)(2,1)} %shard_map.71), channel_id=1, source_target_pairs={{64,0},{72,8},{80,16},{88,24},{96,32},{104,40},{112,48},{120,56},{... | collective-permute-start | bytes 798728 | tf_op jit(solution)/shard_map/ppermute | solution.py:338
  127.7 28.6 %collective-permute-start.23 = (bf16[1040,128]{1,0:T(8,128)(2,1)}, bf16[1040,128]{1,0:T(8,128)(2,1)S(1)}, u32[]{:S(2)}, u32[]{:S(2)}) collective-permute-start(bf16[1040,128]{1,0:T(8,128)(2,1)} %get-tuple-element.61), channel_id=1, source_target_pairs={{8,12},{9,13},{10,14},{11,15},{12,8},{13,9},{14,10},{15,11},{24,28... | collective-permute-start | bytes 798728 | tf_op jit(solution)/shard_map/ppermute | solution.py:336
  133.9 24.3 %collective-permute-start.16 = (bf16[1040,128]{1,0:T(8,128)(2,1)}, bf16[1040,128]{1,0:T(8,128)(2,1)S(1)}, u32[]{:S(2)}, u32[]{:S(2)}) collective-permute-start(bf16[1040,128]{1,0:T(8,128)(2,1)} %get-tuple-element.54), channel_id=1, source_target_pairs={{0,4},{1,5},{2,6},{3,7},{4,0},{5,1},{6,2},{7,3},{16,20},{17,21},{1... | collective-permute-start | bytes 798728 | tf_op jit(solution)/shard_map/ppermute | solution.py:334
where the time goes:
time: 160 us
  waiting for transfers between devices  60.7 us (38%)
  starting transfers between devices  48.9 us (31%)
  Pallas kernels  34.1 us (21%)
  matrix products  15.2 us (10%)
    pallas_call x16, Pallas kernels, call(): pl.pallas_call(kernel, out_shape=outs, in_specs=[SMEM] * scalars + [VMEM]...  34.1 us
    ppermute x1, waiting for transfers between devices, statistics(): grads_in_later = lax.ppermute(grads, 'layer', moves(0, 1))  22.6 us
    ppermute x4, waiting for transfers between devices, first(): lax.ppermute(minus, 'dp', ring[1])  16.5 us
    dot_general x4, matrix products, inner_tokens(): lax.dot_general(left, right, (((0,), (0,)), ((), ())), preferred_element_...  15.2 us
    ppermute x1, waiting for transfers between devices, statistics(): in_v2 = lax.ppermute(out_v2, ('layer', 'dp'), list(across(1)))  10.2 us
    ppermute x4, starting transfers between devices, first(): lax.ppermute(plus, 'dp', ring[0])  9.41 us
    ppermute x1, starting transfers between devices, statistics(): in_u2 = lax.ppermute(out_u2, 'dp', flip)  7.18 us
    ppermute x1, waiting for transfers between devices, statistics(): in_u1 = lax.ppermute(out_u1, 'dp', flip)  6.41 us
  transfers between devices with their start and end apart: 25, of which 9 were waited for; matrix products, arithmetic and copies ran while one was open for 10% of the time, Pallas kernels for 20%

commit v1 on v0

--- a/solution.py
+++ b/solution.py
@@ -175,7 +175,11 @@
     kept[...] = both[pl.ds(rows_of(half), BLK), :]
 
 
-def same_kernel(at, before, kept, same):
+def third_kernel_away(
+    at, total, left1, right1, left2, right2, before, kept, message, same, both
+):
+    third_kernel(at, total, left1, right1, left2, right2, kept, message, both)
+
     @pl.when(at[2] == 0)
     def _():
         send_rows(kept, 0, same)
@@ -306,35 +310,41 @@
             lax.ppermute(minus, "dp", ring[1]),
         )
 
-    def third(state):
+    def third(state, before=None):
         cols = state[0].shape[1]
         outs = (jax.ShapeDtypeStruct((BLK, cols), f32), message_shape(1, cols))
         scratch = (pltpu.VMEM((2 * BLK, cols), f32),)
-        return call(third_kernel, (at,) + state, outs, scratch)
-
-    acts_in = lax.ppermute(acts, "layer", moves(0, -1))
-    grads_in = lax.ppermute(grads, "layer", moves(1, 1))
+        if before is None:
+            return call(third_kernel, (at,) + state, outs, scratch)
+        return call(
+            third_kernel_away, (at,) + state + (before,),
+            outs + (message_shape(1, cols),), scratch,
+        )
+
+    lead = jnp.where(even, acts, grads)
+    lead_in = lax.ppermute(lead, "layer", moves(0, -1) + moves(1, 1))
     u1 = first(inner_tokens(acts, acts))
     u2 = first(inner_tokens(grads, grads))
+    token = u1[1]
     u1 = second(u1)
-    grads_in_later = lax.ppermute(grads, "layer", moves(0, 1))
-    acts_in_later = lax.ppermute(acts, "layer", moves(1, -1))
-    v1 = inner_tokens(jnp.where(even, acts, grads_in), jnp.where(even, acts_in, grads))
+    acts_again, grads_again, _ = lax.optimization_barrier((acts, grads, token))
+    follow = jnp.where(even, grads_again, acts_again)
+    follow_in = lax.ppermute(follow, "layer", moves(0, 1) + moves(1, -1))
+    v1 = inner_tokens(jnp.where(even, lead, lead_in), jnp.where(even, lead_in, lead))
     v1 = first(v1)
     u2 = second(u2)
     kept_u1, out_u1 = third(u1)
     in_u1 = lax.ppermute(out_u1, "dp", flip)
     v1 = second(v1)
-    v2 = inner_tokens(jnp.where(even, grads_in_later, acts), jnp.where(even, grads, acts_in_later))
+    v2 = inner_tokens(jnp.where(even, follow_in, follow), jnp.where(even, follow, follow_in))
     v2 = first(v2)
     kept_u2, out_u2 = third(u2)
     in_u2 = lax.ppermute(out_u2, "dp", flip)
     v2 = second(v2)
     kept_v1, out_v1 = third(v1)
     in_v1 = lax.ppermute(out_v1, ("layer", "dp"), list(across(0)))
-    kept_v2, out_v2 = third(v2)
+    kept_v2, out_v2, same = third(v2, kept_v1)
     in_v2 = lax.ppermute(out_v2, ("layer", "dp"), list(across(1)))
-    same = call(same_kernel, (at, kept_v1, kept_v2), (message_shape(1, width),))[0]
     same_in = lax.ppermute(same, "layer", down)
 
     out_shape = jax.ShapeDtypeStruct((BLK, width), f32)

time: 160 us -> 153 us (0.956)
  the two profiles are of different devices: /device:TPU:14 before, /device:TPU:10 now
where the time goes in v1:
time: 153 us
  waiting for transfers between devices  57.2 us (37%)
  starting transfers between devices  47.2 us (31%)
  Pallas kernels  32.2 us (21%)
  matrix products  12.1 us (8%)
  other arithmetic  3.61 us (2%)
    pallas_call x15, Pallas kernels, call(): pl.pallas_call(kernel, out_shape=outs, in_specs=[SMEM] * scalars + [VMEM]...  32.2 us
    ppermute x1, waiting for transfers between devices, statistics(): lead_in = lax.ppermute(lead, 'layer', moves(0, -1) + moves(1, 1))  23.3 us
    dot_general x4, matrix products, inner_tokens(): lax.dot_general(left, right, (((0,), (0,)), ((), ())), preferred_element_...  12.1 us
    ppermute x4, starting transfers between devices, second(): lax.ppermute(minus, 'dp', ring[1])  11.8 us
    ppermute x1, waiting for transfers between devices, statistics(): in_v1 = lax.ppermute(out_v1, ('layer', 'dp'), list(across(0)))  9.75 us
    ppermute x1, waiting for transfers between devices, statistics(): in_v2 = lax.ppermute(out_v2, ('layer', 'dp'), list(across(1)))  8.51 us
    ppermute x4, waiting for transfers between devices, first(): lax.ppermute(plus, 'dp', ring[0])  7.98 us
    ppermute x1, starting transfers between devices, statistics(): in_v1 = lax.ppermute(out_v1, ('layer', 'dp'), list(across(0)))  7.82 us
  transfers between devices with their start and end apart: 23, of which 8 were waited for; matrix products, arithmetic and copies ran while one was open for 8% of the time, Pallas kernels for 20%

profile of v1, /device:TPU:10, one launch (start us, length us, event | category | flops | bytes accessed | tf_op | source)
XLA Modules:
  0.0 153.2 jit_solution(5780637693703602643)
XLA Ops:
  0.6 3.3 %broadcast_select_fusion.1 = bf16[1024,1024]{1,0:T(8,128)(2,1)} fusion(bf16[1024,1024]{1,0:T(8,128)(2,1)} %param.2, bf16[1024,1024]{1,0:T(8,128)(2,1)} %param.3, pred[]{:T(512)S(6)} %eq.3), kind=kLoop, calls=%fused_computation.9 | loop fusion | flops 1048576 | bytes 6291457 | tf_op jit(solution)/shard_map/jit(_where)/select_n | solution.py:324
  4.0 2.3 %collective-permute-start.10 = (bf16[1024,1024]{1,0:T(8,128)(2,1)}, bf16[1024,1024]{1,0:T(8,128)(2,1)}, u32[]{:S(2)}, u32[]{:S(2)}) collective-permute-start(bf16[1024,1024]{1,0:T(8,128)(2,1)} %broadcast_select_fusion.1), channel_id=1, source_target_pairs={{64,0},{80,16},{96,32},{112,48},{128,64},{144,80},{160,96},{176,11... | collective-permute-start | bytes 6291464 | tf_op jit(solution)/shard_map/ppermute | solution.py:325
  6.3 0.1 pad_add_fusion.at
  6.4 2.4 %fusion.8.total = f32[1024,1024]{1,0:T(8,128)S(1)} fusion(bf16[1024,1024]{1,0:T(8,128)(2,1)S(1)} %copy-done), kind=kOutput, calls=%fused_computation.11 | convolution fusion | flops 2147483648 | bytes 6291456 | tf_op jit(solution)/shard_map/dot_general | solution.py:247
  8.8 0.0 copy-start.1
  8.8 2.7 %shard_map.57 = (bf16[2064,128]{1,0:T(8,128)(2,1)S(1)}, bf16[2064,128]{1,0:T(8,128)(2,1)S(1)}, f32[8,128]{1,0:T(8,128)S(1)}) custom-call(s32[3]{0:T(128)S(1)} %pad_add_fusion.at, f32[1024,1024]{1,0:T(8,128)S(1)} %fusion.8.total), custom_call_target="tpu_custom_call" | custom-call | tf_op jit(solution)/shard_map/pallas_call | solution.py:229
  11.5 0.2 broadcast_select_fusion
  11.7 3.5 %collective-permute-start.16 = (bf16[1024,1024]{1,0:T(8,128)(2,1)S(1)}, bf16[1024,1024]{1,0:T(8,128)(2,1)S(1)}, u32[]{:S(2)}, u32[]{:S(2)}) collective-permute-start(bf16[1024,1024]{1,0:T(8,128)(2,1)S(1)} %broadcast_select_fusion), channel_id=1, source_target_pairs={{0,64},{16,80},{32,96},{48,112},{64,128},{80,144},{96,160},{112,17... | collective-permute-start | bytes 6291464 | tf_op jit(solution)/shard_map/ppermute | solution.py:332
  15.2 1.6 %collective-permute-start = (bf16[2064,128]{1,0:T(8,128)(2,1)S(1)}, bf16[2064,128]{1,0:T(8,128)(2,1)S(1)}, u32[]{:S(2)}, u32[]{:S(2)}) collective-permute-start(bf16[2064,128]{1,0:T(8,128)(2,1)S(1)} %get-tuple-element.37), channel_id=1, source_target_pairs={{0,1},{1,2},{2,3},{3,0},{4,5},{5,6},{6,7},{7,4},{8,9},{9,10},{10,1... | collective-permute-start | bytes 1585160 | tf_op jit(solution)/shard_map/ppermute | solution.py:296
  16.8 0.5 collective-permute-start.1
  17.3 2.4 %fusion.9.total = f32[1024,1024]{1,0:T(8,128)S(1)} fusion(bf16[1024,1024]{1,0:T(8,128)(2,1)S(1)} %copy-done.1), kind=kOutput, calls=%fused_computation.12 | convolution fusion | flops 2147483648 | bytes 6291456 | tf_op jit(solution)/shard_map/dot_general | solution.py:247
  19.8 2.7 %shard_map.61 = (bf16[2064,128]{1,0:T(8,128)(2,1)S(1)}, bf16[2064,128]{1,0:T(8,128)(2,1)S(1)}, f32[8,128]{1,0:T(8,128)S(1)}) custom-call(s32[3]{0:T(128)S(1)} %pad_add_fusion.at, f32[1024,1024]{1,0:T(8,128)S(1)} %fusion.9.total), custom_call_target="tpu_custom_call" | custom-call | tf_op jit(solution)/shard_map/pallas_call | solution.py:229
  22.5 1.6 %collective-permute-start.5 = (bf16[2064,128]{1,0:T(8,128)(2,1)S(1)}, bf16[2064,128]{1,0:T(8,128)(2,1)S(1)}, u32[]{:S(2)}, u32[]{:S(2)}) collective-permute-start(bf16[2064,128]{1,0:T(8,128)(2,1)S(1)} %get-tuple-element.44), channel_id=1, source_target_pairs={{0,1},{1,2},{2,3},{3,0},{4,5},{5,6},{6,7},{7,4},{8,9},{9,10},{10,1... | collective-permute-start | bytes 1585160 | tf_op jit(solution)/shard_map/ppermute | solution.py:296
  24.0 23.3 %collective-permute-done.10 = bf16[1024,1024]{1,0:T(8,128)(2,1)} collective-permute-done((bf16[1024,1024]{1,0:T(8,128)(2,1)}, bf16[1024,1024]{1,0:T(8,128)(2,1)}, u32[]{:S(2)}, u32[]{:S(2)}) %collective-permute-start.10) | collective-permute-done | bytes 2097184 | tf_op jit(solution)/shard_map/ppermute | solution.py:325
  47.4 0.6 collective-permute-start.6
  48.0 4.7 %fusion.3.total = f32[1024,1024]{1,0:T(8,128)S(1)} fusion(bf16[1024,1024]{1,0:T(8,128)(2,1)} %collective-permute-done.10, bf16[1024,1024]{1,0:T(8,128)(2,1)} %broadcast_select_fusion.1, pred[]{:T(512)S(6)} %eq.3), kind=kOutput, calls=%fused_computation.3 | convolution fusion | flops 2149580800 | bytes 8388609 | tf_op jit(solution)/shard_map/dot_general | solution.py:247
  52.7 2.7 %shard_map.65 = (bf16[2064,128]{1,0:T(8,128)(2,1)S(1)}, bf16[2064,128]{1,0:T(8,128)(2,1)S(1)}, f32[8,128]{1,0:T(8,128)S(1)}) custom-call(s32[3]{0:T(128)S(1)} %pad_add_fusion.at, f32[1024,1024]{1,0:T(8,128)S(1)} %fusion.3.total), custom_call_target="tpu_custom_call" | custom-call | tf_op jit(solution)/shard_map/pallas_call | solution.py:229
  55.4 0.0 collective-permute-done.from_left.left1
  55.4 1.7 %collective-permute-start.11 = (bf16[2064,128]{1,0:T(8,128)(2,1)S(1)}, bf16[2064,128]{1,0:T(8,128)(2,1)S(1)}, u32[]{:S(2)}, u32[]{:S(2)}) collective-permute-start(bf16[2064,128]{1,0:T(8,128)(2,1)S(1)} %get-tuple-element.51), channel_id=1, source_target_pairs={{0,1},{1,2},{2,3},{3,0},{4,5},{5,6},{6,7},{7,4},{8,9},{9,10},{10,1... | collective-permute-start | bytes 1585160 | tf_op jit(solution)/shard_map/ppermute | solution.py:296
  57.1 0.0 collective-permute-done.16
  57.1 1.3 collective-permute-start.12
  58.5 2.5 %fusion.total = f32[1024,1024]{1,0:T(8,128)S(1)} fusion(bf16[1024,1024]{1,0:T(8,128)(2,1)S(1)} %broadcast_select_fusion, bf16[1024,1024]{1,0:T(8,128)(2,1)S(1)} %collective-permute-done.16, pred[]{:T(512)S(6)} %eq.3), kind=kOutput, calls=%fused_computation | convolution fusion | flops 2149580800 | bytes 8388609 | tf_op jit(solution)/shard_map/dot_general | solution.py:247
  60.9 2.7 %shard_map.68 = (bf16[2064,128]{1,0:T(8,128)(2,1)S(1)}, bf16[2064,128]{1,0:T(8,128)(2,1)S(1)}, f32[8,128]{1,0:T(8,128)S(1)}) custom-call(s32[3]{0:T(128)S(1)} %pad_add_fusion.at, f32[1024,1024]{1,0:T(8,128)S(1)} %fusion.total), custom_call_target="tpu_custom_call" | custom-call | tf_op jit(solution)/shard_map/pallas_call | solution.py:229
  63.6 0.0 collective-permute-done.1.from_right.right1
  63.6 0.8 collective-permute-start.17
  64.4 2.6 %collective-permute-start.18 = (bf16[2064,128]{1,0:T(8,128)(2,1)S(1)}, bf16[2064,128]{1,0:T(8,128)(2,1)S(1)}, u32[]{:S(2)}, u32[]{:S(2)}) collective-permute-start(bf16[2064,128]{1,0:T(8,128)(2,1)S(1)} %get-tuple-element.61), channel_id=1, source_target_pairs={{0,3},{1,0},{2,1},{3,2},{4,7},{5,4},{6,5},{7,6},{8,11},{9,8},{10,9... | collective-permute-start | bytes 1585160 | tf_op jit(solution)/shard_map/ppermute | solution.py:297
  66.9 1.5 shard_map.58
  68.5 0.1 collective-permute-start.2
  68.6 1.5 shard_map.62
  70.1 1.1 collective-permute-done.11.from_left.left1
  71.2 3.0 %collective-permute-start.3 = (bf16[1040,128]{1,0:T(8,128)(2,1)S(1)}, bf16[1040,128]{1,0:T(8,128)(2,1)S(1)}, u32[]{:S(2)}, u32[]{:S(2)}) collective-permute-start(bf16[1040,128]{1,0:T(8,128)(2,1)S(1)} %get-tuple-element.41), channel_id=1, source_target_pairs={{0,3},{1,0},{2,1},{3,2},{4,7},{5,4},{6,5},{7,6},{8,11},{9,8},{10,9... | collective-permute-start | bytes 798728 | tf_op jit(solution)/shard_map/ppermute | solution.py:310
  74.2 0.0 collective-permute-done.12.from_right.right1
  74.2 0.0 collective-permute-start.7
  74.2 1.5 shard_map.66
  75.7 6.8 %collective-permute-done.17.from_left.left1 = bf16[2064,128]{1,0:T(8,128)(2,1)S(1)} collective-permute-done((bf16[2064,128]{1,0:T(8,128)(2,1)S(1)}, bf16[2064,128]{1,0:T(8,128)(2,1)S(1)}, u32[]{:S(2)}, u32[]{:S(2)}) %collective-permute-start.17) | collective-permute-done | bytes 528416 | tf_op jit(solution)/shard_map/ppermute | solution.py:296
  82.5 3.0 %collective-permute-start.8 = (bf16[1040,128]{1,0:T(8,128)(2,1)S(1)}, bf16[1040,128]{1,0:T(8,128)(2,1)S(1)}, u32[]{:S(2)}, u32[]{:S(2)}) collective-permute-start(bf16[1040,128]{1,0:T(8,128)(2,1)S(1)} %get-tuple-element.48), channel_id=1, source_target_pairs={{0,3},{1,0},{2,1},{3,2},{4,7},{5,4},{6,5},{7,6},{8,11},{9,8},{10,9... | collective-permute-start | bytes 798728 | tf_op jit(solution)/shard_map/ppermute | solution.py:310
  85.5 0.0 collective-permute-done.18.from_right.right1
  85.5 0.0 collective-permute-start.13
  85.5 1.5 shard_map.69
  87.0 1.2 collective-permute-done.2.left2
  88.2 3.0 %collective-permute-start.14 = (bf16[1040,128]{1,0:T(8,128)(2,1)S(1)}, bf16[1040,128]{1,0:T(8,128)(2,1)S(1)}, u32[]{:S(2)}, u32[]{:S(2)}) collective-permute-start(bf16[1040,128]{1,0:T(8,128)(2,1)S(1)} %get-tuple-element.55), channel_id=1, source_target_pairs={{0,3},{1,0},{2,1},{3,2},{4,7},{5,4},{6,5},{7,6},{8,11},{9,8},{10,9... | collective-permute-start | bytes 798728 | tf_op jit(solution)/shard_map/ppermute | solution.py:310
  91.2 2.7 %collective-permute-done.7.left2 = bf16[1040,128]{1,0:T(8,128)(2,1)S(1)} collective-permute-done((bf16[1040,128]{1,0:T(8,128)(2,1)S(1)}, bf16[1040,128]{1,0:T(8,128)(2,1)S(1)}, u32[]{:S(2)}, u32[]{:S(2)}) %collective-permute-start.7) | collective-permute-done | bytes 266272 | tf_op jit(solution)/shard_map/ppermute | solution.py:309
  93.9 3.0 %collective-permute-start.20 = (bf16[1040,128]{1,0:T(8,128)(2,1)S(1)}, bf16[1040,128]{1,0:T(8,128)(2,1)S(1)}, u32[]{:S(2)}, u32[]{:S(2)}) collective-permute-start(bf16[1040,128]{1,0:T(8,128)(2,1)S(1)} %get-tuple-element.64), channel_id=1, source_target_pairs={{0,3},{1,0},{2,1},{3,2},{4,7},{5,4},{6,5},{7,6},{8,11},{9,8},{10,9... | collective-permute-start | bytes 798728 | tf_op jit(solution)/shard_map/ppermute | solution.py:310
  96.9 2.7 %shard_map.59 = (f32[128,1024]{1,0:T(8,128)S(1)}, bf16[1040,128]{1,0:T(8,128)(2,1)}) custom-call(s32[3]{0:T(128)S(1)} %pad_add_fusion.at, f32[1024,1024]{1,0:T(8,128)S(1)} %fusion.8.total, bf16[2064,128]{1,0:T(8,128)(2,1)S(1)} %collective-permute-done.from_left.left1, bf16[2064,128]{1,0:T(8,128)(2,1)S(1)} %collective-permute-done.1.from_right.right1, ...), custom_call_target="tpu_custom_call" | custom-call | tf_op jit(solution)/shard_map/pallas_call | solution.py:229
  99.6 0.0 collective-permute-done.8.right2
  99.6 7.2 %collective-permute-start.4 = (bf16[1040,128]{1,0:T(8,128)(2,1)}, bf16[1040,128]{1,0:T(8,128)(2,1)S(1)}, u32[]{:S(2)}, u32[]{:S(2)}) collective-permute-start(bf16[1040,128]{1,0:T(8,128)(2,1)} %get-tuple-element.43), channel_id=1, source_target_pairs={{0,4},{1,5},{2,6},{3,7},{4,0},{5,1},{6,2},{7,3},{8,12},{9,13},{10,... | collective-permute-start | bytes 798728 | tf_op jit(solution)/shard_map/ppermute | solution.py:337
  106.8 2.7 %shard_map.63 = (f32[128,1024]{1,0:T(8,128)S(1)}, bf16[1040,128]{1,0:T(8,128)(2,1)}) custom-call(s32[3]{0:T(128)S(1)} %pad_add_fusion.at, f32[1024,1024]{1,0:T(8,128)S(1)} %fusion.9.total, bf16[2064,128]{1,0:T(8,128)(2,1)S(1)} %collective-permute-done.5.from_left.left1, bf16[2064,128]{1,0:T(8,128)(2,1)S(1)} %collective-permute-done.6.from_right.right1, ...), custom_call_target="tpu_custom_call" | custom-call | tf_op jit(solution)/shard_map/pallas_call | solution.py:229
  109.5 0.0 collective-permute-done.13.left2
  109.5 0.0 collective-permute-start.9
  109.5 0.0 collective-permute-done.14.right2
  109.5 2.7 %shard_map.67 = (f32[128,1024]{1,0:T(8,128)S(1)}, bf16[1040,128]{1,0:T(8,128)(2,1)}) custom-call(s32[3]{0:T(128)S(1)} %pad_add_fusion.at, f32[1024,1024]{1,0:T(8,128)S(1)} %fusion.3.total, bf16[2064,128]{1,0:T(8,128)(2,1)S(1)} %collective-permute-done.11.from_left.left1, bf16[2064,128]{1,0:T(8,128)(2,1)S(1)} %collective-permute-done.12.from_right.right1, ...), custom_call_target="tpu_custom_call" | custom-call | tf_op jit(solution)/shard_map/pallas_call | solution.py:229
  112.3 7.8 %collective-permute-start.15 = (bf16[1040,128]{1,0:T(8,128)(2,1)}, bf16[1040,128]{1,0:T(8,128)(2,1)S(1)}, u32[]{:S(2)}, u32[]{:S(2)}) collective-permute-start(bf16[1040,128]{1,0:T(8,128)(2,1)} %get-tuple-element.57), channel_id=1, source_target_pairs={{0,4},{1,5},{2,6},{3,7},{4,0},{5,1},{6,2},{7,3},{16,20},{17,21},{1... | collective-permute-start | bytes 798728 | tf_op jit(solution)/shard_map/ppermute | solution.py:345
  120.1 0.0 collective-permute-done.19.left2
  120.1 3.3 %shard_map.70 = (f32[128,1024]{1,0:T(8,128)S(1)}, bf16[1040,128]{1,0:T(8,128)(2,1)}, bf16[1040,128]{1,0:T(8,128)(2,1)}) custom-call(s32[3]{0:T(128)S(1)} %pad_add_fusion.at, f32[1024,1024]{1,0:T(8,128)S(1)} %fusion.total, bf16[2064,128]{1,0:T(8,128)(2,1)S(1)} %collective-permute-done.17.from_left.left1, ...), custom_call_target="tpu_custom_call" | custom-call | tf_op jit(solution)/shard_map/pallas_call | solution.py:229
  123.4 1.9 %collective-permute-start.21 = (bf16[1040,128]{1,0:T(8,128)(2,1)}, bf16[1040,128]{1,0:T(8,128)(2,1)S(1)}, u32[]{:S(2)}, u32[]{:S(2)}) collective-permute-start(bf16[1040,128]{1,0:T(8,128)(2,1)} %get-tuple-element.66), channel_id=1, source_target_pairs={{8,12},{9,13},{10,14},{11,15},{12,8},{13,9},{14,10},{15,11},{24,28... | collective-permute-start | bytes 798728 | tf_op jit(solution)/shard_map/ppermute | solution.py:347
  125.4 1.9 %collective-permute-start.22 = (bf16[1040,128]{1,0:T(8,128)(2,1)}, bf16[1040,128]{1,0:T(8,128)(2,1)S(1)}, u32[]{:S(2)}, u32[]{:S(2)}) collective-permute-start(bf16[1040,128]{1,0:T(8,128)(2,1)} %get-tuple-element.67), channel_id=1, source_target_pairs={{64,0},{72,8},{80,16},{88,24},{96,32},{104,40},{112,48},{120,56},{... | collective-permute-start | bytes 798728 | tf_op jit(solution)/shard_map/ppermute | solution.py:348
  127.3 0.0 collective-permute-done.4.message
  127.3 1.1 shard_map.60
  128.4 3.6 %collective-permute-done.9.message = bf16[1040,128]{1,0:T(8,128)(2,1)S(1)} collective-permute-done((bf16[1040,128]{1,0:T(8,128)(2,1)}, bf16[1040,128]{1,0:T(8,128)(2,1)S(1)}, u32[]{:S(2)}, u32[]{:S(2)}) %collective-permute-start.9) | collective-permute-done | bytes 266272 | tf_op jit(solution)/shard_map/ppermute | solution.py:342
  132.1 1.1 shard_map.64
  133.2 9.8 %collective-permute-done.15.other1 = bf16[1040,128]{1,0:T(8,128)(2,1)S(1)} collective-permute-done((bf16[1040,128]{1,0:T(8,128)(2,1)}, bf16[1040,128]{1,0:T(8,128)(2,1)S(1)}, u32[]{:S(2)}, u32[]{:S(2)}) %collective-permute-start.15) | collective-permute-done | bytes 266272 | tf_op jit(solution)/shard_map/ppermute | solution.py:345
  142.9 8.5 %collective-permute-done.21.other2 = bf16[1040,128]{1,0:T(8,128)(2,1)S(1)} collective-permute-done((bf16[1040,128]{1,0:T(8,128)(2,1)}, bf16[1040,128]{1,0:T(8,128)(2,1)S(1)}, u32[]{:S(2)}, u32[]{:S(2)}) %collective-permute-start.21) | collective-permute-done | bytes 266272 | tf_op jit(solution)/shard_map/ppermute | solution.py:347
  151.4 0.0 collective-permute-done.22.same
  151.4 1.8 %shard_map.71 = (f32[128,1024]{1,0:T(8,128)}, f32[128,1024]{1,0:T(8,128)}) custom-call(f32[1]{0:T(128)} %bitcast.3.scale, s32[1]{0:T(128)} %bitcast.2.at, f32[128,1024]{1,0:T(8,128)S(1)} %get-tuple-element.56.before.kept1, bf16[1040,128]{1,0:T(8,128)(2,1)S(1)} %collective-permute-done.15.other1, f32[128,1024]{1,0:T(8,128)S(1)} %get-tuple-element.65.kept2, ...), custom_call_target="tpu_custom_call" | custom-call | tf_op jit(solution)/shard_map/pallas_call | solution.py:229
  (8 shorter events, 0.0 us)
Async XLA Ops:
  0.6 5.8 %copy-start = (bf16[1024,1024]{1,0:T(8,128)(2,1)S(1)}, bf16[1024,1024]{1,0:T(8,128)(2,1)}, u32[]{:S(2)}) copy-start(bf16[1024,1024]{1,0:T(8,128)(2,1)} %param.2) | copy-start | bytes 6291460
  4.0 43.4 %collective-permute-start.10 = (bf16[1024,1024]{1,0:T(8,128)(2,1)}, bf16[1024,1024]{1,0:T(8,128)(2,1)}, u32[]{:S(2)}, u32[]{:S(2)}) collective-permute-start(bf16[1024,1024]{1,0:T(8,128)(2,1)} %broadcast_select_fusion.1), channel_id=1, source_target_pairs={{64,0},{80,16},{96,32},{112,48},{128,64},{144,80},{160,96},{176,11... | collective-permute-start | bytes 6291464 | tf_op jit(solution)/shard_map/ppermute | solution.py:325
  8.8 2.7 %copy-start.1 = (bf16[1024,1024]{1,0:T(8,128)(2,1)S(1)}, bf16[1024,1024]{1,0:T(8,128)(2,1)}, u32[]{:S(2)}) copy-start(bf16[1024,1024]{1,0:T(8,128)(2,1)} %param.3) | copy-start | bytes 6291460
  11.7 45.4 %collective-permute-start.16 = (bf16[1024,1024]{1,0:T(8,128)(2,1)S(1)}, bf16[1024,1024]{1,0:T(8,128)(2,1)S(1)}, u32[]{:S(2)}, u32[]{:S(2)}) collective-permute-start(bf16[1024,1024]{1,0:T(8,128)(2,1)S(1)} %broadcast_select_fusion), channel_id=1, source_target_pairs={{0,64},{16,80},{32,96},{48,112},{64,128},{80,144},{96,160},{112,17... | collective-permute-start | bytes 6291464 | tf_op jit(solution)/shard_map/ppermute | solution.py:332
  15.2 40.1 %collective-permute-start = (bf16[2064,128]{1,0:T(8,128)(2,1)S(1)}, bf16[2064,128]{1,0:T(8,128)(2,1)S(1)}, u32[]{:S(2)}, u32[]{:S(2)}) collective-permute-start(bf16[2064,128]{1,0:T(8,128)(2,1)S(1)} %get-tuple-element.37), channel_id=1, source_target_pairs={{0,1},{1,2},{2,3},{3,0},{4,5},{5,6},{6,7},{7,4},{8,9},{9,10},{10,1... | collective-permute-start | bytes 1585160 | tf_op jit(solution)/shard_map/ppermute | solution.py:296
  16.8 46.8 %collective-permute-start.1 = (bf16[2064,128]{1,0:T(8,128)(2,1)S(1)}, bf16[2064,128]{1,0:T(8,128)(2,1)S(1)}, u32[]{:S(2)}, u32[]{:S(2)}) collective-permute-start(bf16[2064,128]{1,0:T(8,128)(2,1)S(1)} %get-tuple-element.38), channel_id=1, source_target_pairs={{0,3},{1,0},{2,1},{3,2},{4,7},{5,4},{6,5},{7,6},{8,11},{9,8},{10,9... | collective-permute-start | bytes 1585160 | tf_op jit(solution)/shard_map/ppermute | solution.py:297
  22.5 41.9 %collective-permute-start.5 = (bf16[2064,128]{1,0:T(8,128)(2,1)S(1)}, bf16[2064,128]{1,0:T(8,128)(2,1)S(1)}, u32[]{:S(2)}, u32[]{:S(2)}) collective-permute-start(bf16[2064,128]{1,0:T(8,128)(2,1)S(1)} %get-tuple-element.44), channel_id=1, source_target_pairs={{0,1},{1,2},{2,3},{3,0},{4,5},{5,6},{6,7},{7,4},{8,9},{9,10},{10,1... | collective-permute-start | bytes 1585160 | tf_op jit(solution)/shard_map/ppermute | solution.py:296
  47.4 21.1 %collective-permute-start.6 = (bf16[2064,128]{1,0:T(8,128)(2,1)S(1)}, bf16[2064,128]{1,0:T(8,128)(2,1)S(1)}, u32[]{:S(2)}, u32[]{:S(2)}) collective-permute-start(bf16[2064,128]{1,0:T(8,128)(2,1)S(1)} %get-tuple-element.45), channel_id=1, source_target_pairs={{0,3},{1,0},{2,1},{3,2},{4,7},{5,4},{6,5},{7,6},{8,11},{9,8},{10,9... | collective-permute-start | bytes 1585160 | tf_op jit(solution)/shard_map/ppermute | solution.py:297
  55.4 15.8 %collective-permute-start.11 = (bf16[2064,128]{1,0:T(8,128)(2,1)S(1)}, bf16[2064,128]{1,0:T(8,128)(2,1)S(1)}, u32[]{:S(2)}, u32[]{:S(2)}) collective-permute-start(bf16[2064,128]{1,0:T(8,128)(2,1)S(1)} %get-tuple-element.51), channel_id=1, source_target_pairs={{0,1},{1,2},{2,3},{3,0},{4,5},{5,6},{6,7},{7,4},{8,9},{9,10},{10,1... | collective-permute-start | bytes 1585160 | tf_op jit(solution)/shard_map/ppermute | solution.py:296
  57.1 17.1 %collective-permute-start.12 = (bf16[2064,128]{1,0:T(8,128)(2,1)S(1)}, bf16[2064,128]{1,0:T(8,128)(2,1)S(1)}, u32[]{:S(2)}, u32[]{:S(2)}) collective-permute-start(bf16[2064,128]{1,0:T(8,128)(2,1)S(1)} %get-tuple-element.52), channel_id=1, source_target_pairs={{0,3},{1,0},{2,1},{3,2},{4,7},{5,4},{6,5},{7,6},{8,11},{9,8},{10,9... | collective-permute-start | bytes 1585160 | tf_op jit(solution)/shard_map/ppermute | solution.py:297
  63.6 18.9 %collective-permute-start.17 = (bf16[2064,128]{1,0:T(8,128)(2,1)S(1)}, bf16[2064,128]{1,0:T(8,128)(2,1)S(1)}, u32[]{:S(2)}, u32[]{:S(2)}) collective-permute-start(bf16[2064,128]{1,0:T(8,128)(2,1)S(1)} %get-tuple-element.60), channel_id=1, source_target_pairs={{0,1},{1,2},{2,3},{3,0},{4,5},{5,6},{6,7},{7,4},{8,9},{9,10},{10,1... | collective-permute-start | bytes 1585160 | tf_op jit(solution)/shard_map/ppermute | solution.py:296
  64.4 21.1 %collective-permute-start.18 = (bf16[2064,128]{1,0:T(8,128)(2,1)S(1)}, bf16[2064,128]{1,0:T(8,128)(2,1)S(1)}, u32[]{:S(2)}, u32[]{:S(2)}) collective-permute-start(bf16[2064,128]{1,0:T(8,128)(2,1)S(1)} %get-tuple-element.61), channel_id=1, source_target_pairs={{0,3},{1,0},{2,1},{3,2},{4,7},{5,4},{6,5},{7,6},{8,11},{9,8},{10,9... | collective-permute-start | bytes 1585160 | tf_op jit(solution)/shard_map/ppermute | solution.py:297
  68.5 19.8 %collective-permute-start.2 = (bf16[1040,128]{1,0:T(8,128)(2,1)S(1)}, bf16[1040,128]{1,0:T(8,128)(2,1)S(1)}, u32[]{:S(2)}, u32[]{:S(2)}) collective-permute-start(bf16[1040,128]{1,0:T(8,128)(2,1)S(1)} %get-tuple-element.40), channel_id=1, source_target_pairs={{0,1},{1,2},{2,3},{3,0},{4,5},{5,6},{6,7},{7,4},{8,9},{9,10},{10,1... | collective-permute-start | bytes 798728 | tf_op jit(solution)/shard_map/ppermute | solution.py:309
  71.2 20.0 %collective-permute-start.3 = (bf16[1040,128]{1,0:T(8,128)(2,1)S(1)}, bf16[1040,128]{1,0:T(8,128)(2,1)S(1)}, u32[]{:S(2)}, u32[]{:S(2)}) collective-permute-start(bf16[1040,128]{1,0:T(8,128)(2,1)S(1)} %get-tuple-element.41), channel_id=1, source_target_pairs={{0,3},{1,0},{2,1},{3,2},{4,7},{5,4},{6,5},{7,6},{8,11},{9,8},{10,9... | collective-permute-start | bytes 798728 | tf_op jit(solution)/shard_map/ppermute | solution.py:310
  74.2 19.8 %collective-permute-start.7 = (bf16[1040,128]{1,0:T(8,128)(2,1)S(1)}, bf16[1040,128]{1,0:T(8,128)(2,1)S(1)}, u32[]{:S(2)}, u32[]{:S(2)}) collective-permute-start(bf16[1040,128]{1,0:T(8,128)(2,1)S(1)} %get-tuple-element.47), channel_id=1, source_target_pairs={{0,1},{1,2},{2,3},{3,0},{4,5},{5,6},{6,7},{7,4},{8,9},{9,10},{10,1... | collective-permute-start | bytes 798728 | tf_op jit(solution)/shard_map/ppermute | solution.py:309
  82.5 17.1 %collective-permute-start.8 = (bf16[1040,128]{1,0:T(8,128)(2,1)S(1)}, bf16[1040,128]{1,0:T(8,128)(2,1)S(1)}, u32[]{:S(2)}, u32[]{:S(2)}) collective-permute-start(bf16[1040,128]{1,0:T(8,128)(2,1)S(1)} %get-tuple-element.48), channel_id=1, source_target_pairs={{0,3},{1,0},{2,1},{3,2},{4,7},{5,4},{6,5},{7,6},{8,11},{9,8},{10,9... | collective-permute-start | bytes 798728 | tf_op jit(solution)/shard_map/ppermute | solution.py:310
  85.5 24.0 %collective-permute-start.13 = (bf16[1040,128]{1,0:T(8,128)(2,1)S(1)}, bf16[1040,128]{1,0:T(8,128)(2,1)S(1)}, u32[]{:S(2)}, u32[]{:S(2)}) collective-permute-start(bf16[1040,128]{1,0:T(8,128)(2,1)S(1)} %get-tuple-element.54), channel_id=1, source_target_pairs={{0,1},{1,2},{2,3},{3,0},{4,5},{5,6},{6,7},{7,4},{8,9},{9,10},{10,1... | collective-permute-start | bytes 798728 | tf_op jit(solution)/shard_map/ppermute | solution.py:309
  88.2 21.3 %collective-permute-start.14 = (bf16[1040,128]{1,0:T(8,128)(2,1)S(1)}, bf16[1040,128]{1,0:T(8,128)(2,1)S(1)}, u32[]{:S(2)}, u32[]{:S(2)}) collective-permute-start(bf16[1040,128]{1,0:T(8,128)(2,1)S(1)} %get-tuple-element.55), channel_id=1, source_target_pairs={{0,3},{1,0},{2,1},{3,2},{4,7},{5,4},{6,5},{7,6},{8,11},{9,8},{10,9... | collective-permute-start | bytes 798728 | tf_op jit(solution)/shard_map/ppermute | solution.py:310
  91.2 28.9 %collective-permute-start.19 = (bf16[1040,128]{1,0:T(8,128)(2,1)S(1)}, bf16[1040,128]{1,0:T(8,128)(2,1)S(1)}, u32[]{:S(2)}, u32[]{:S(2)}) collective-permute-start(bf16[1040,128]{1,0:T(8,128)(2,1)S(1)} %get-tuple-element.63), channel_id=1, source_target_pairs={{0,1},{1,2},{2,3},{3,0},{4,5},{5,6},{6,7},{7,4},{8,9},{9,10},{10,1... | collective-permute-start | bytes 798728 | tf_op jit(solution)/shard_map/ppermute | solution.py:309
  93.9 26.2 %collective-permute-start.20 = (bf16[1040,128]{1,0:T(8,128)(2,1)S(1)}, bf16[1040,128]{1,0:T(8,128)(2,1)S(1)}, u32[]{:S(2)}, u32[]{:S(2)}) collective-permute-start(bf16[1040,128]{1,0:T(8,128)(2,1)S(1)} %get-tuple-element.64), channel_id=1, source_target_pairs={{0,3},{1,0},{2,1},{3,2},{4,7},{5,4},{6,5},{7,6},{8,11},{9,8},{10,9... | collective-permute-start | bytes 798728 | tf_op jit(solution)/shard_map/ppermute | solution.py:310
  99.6 27.7 %collective-permute-start.4 = (bf16[1040,128]{1,0:T(8,128)(2,1)}, bf16[1040,128]{1,0:T(8,128)(2,1)S(1)}, u32[]{:S(2)}, u32[]{:S(2)}) collective-permute-start(bf16[1040,128]{1,0:T(8,128)(2,1)} %get-tuple-element.43), channel_id=1, source_target_pairs={{0,4},{1,5},{2,6},{3,7},{4,0},{5,1},{6,2},{7,3},{8,12},{9,13},{10,... | collective-permute-start | bytes 798728 | tf_op jit(solution)/shard_map/ppermute | solution.py:337
  109.5 22.5 %collective-permute-start.9 = (bf16[1040,128]{1,0:T(8,128)(2,1)}, bf16[1040,128]{1,0:T(8,128)(2,1)S(1)}, u32[]{:S(2)}, u32[]{:S(2)}) collective-permute-start(bf16[1040,128]{1,0:T(8,128)(2,1)} %get-tuple-element.50), channel_id=1, source_target_pairs={{0,4},{1,5},{2,6},{3,7},{4,0},{5,1},{6,2},{7,3},{8,12},{9,13},{10,... | collective-permute-start | bytes 798728 | tf_op jit(solution)/shard_map/ppermute | solution.py:342
  112.3 30.6 %collective-permute-start.15 = (bf16[1040,128]{1,0:T(8,128)(2,1)}, bf16[1040,128]{1,0:T(8,128)(2,1)S(1)}, u32[]{:S(2)}, u32[]{:S(2)}) collective-permute-start(bf16[1040,128]{1,0:T(8,128)(2,1)} %get-tuple-element.57), channel_id=1, source_target_pairs={{0,4},{1,5},{2,6},{3,7},{4,0},{5,1},{6,2},{7,3},{16,20},{17,21},{1... | collective-permute-start | bytes 798728 | tf_op jit(solution)/shard_map/ppermute | solution.py:345
  123.4 28.0 %collective-permute-start.21 = (bf16[1040,128]{1,0:T(8,128)(2,1)}, bf16[1040,128]{1,0:T(8,128)(2,1)S(1)}, u32[]{:S(2)}, u32[]{:S(2)}) collective-permute-start(bf16[1040,128]{1,0:T(8,128)(2,1)} %get-tuple-element.66), channel_id=1, source_target_pairs={{8,12},{9,13},{10,14},{11,15},{12,8},{13,9},{14,10},{15,11},{24,28... | collective-permute-start | bytes 798728 | tf_op jit(solution)/shard_map/ppermute | solution.py:347
  125.4 26.1 %collective-permute-start.22 = (bf16[1040,128]{1,0:T(8,128)(2,1)}, bf16[1040,128]{1,0:T(8,128)(2,1)S(1)}, u32[]{:S(2)}, u32[]{:S(2)}) collective-permute-start(bf16[1040,128]{1,0:T(8,128)(2,1)} %get-tuple-element.67), channel_id=1, source_target_pairs={{64,0},{72,8},{80,16},{88,24},{96,32},{104,40},{112,48},{120,56},{... | collective-permute-start | bytes 798728 | tf_op jit(solution)/shard_map/ppermute | solution.py:348
